TPU v7x, 32 devices: a whole 2x2x4 slice. The times are simulated.
32 devices in a mesh: seq: 8 (over z, x), fsdp: 4 (over y, core).
Axes of the slice: x: 2, y: 2, z: 4, core: 2. Of those that a mesh axis runs over, the one named last changes fastest.
Arguments:
- tokens: bfloat16 [4, 1024, 1152], P('fsdp', 'seq'), may hold values from -6 to 6
- cotangent: bfloat16 [4, 1024, 1152], P('fsdp', 'seq'), may hold values from -6 to 6
- attn_norm: bfloat16 [1152], P('fsdp'), may hold values from 0.25 to 1.75
- q_norm: bfloat16 [256], P('fsdp'), may hold values from 0.25 to 1.75
- k_norm: bfloat16 [256], P('fsdp'), may hold values from 0.25 to 1.75
- post_attn_norm: bfloat16 [1152], P('fsdp'), may hold values from 0.25 to 1.75
- ffn_norm: bfloat16 [1152], P('fsdp'), may hold values from 0.25 to 1.75
- post_ffn_norm: bfloat16 [1152], P('fsdp'), may hold values from 0.25 to 1.75
- w_query: bfloat16 [1152, 1024], P('fsdp'), may hold values from -0.1875 to 0.1875
- w_key: bfloat16 [1152, 256], P('fsdp'), may hold values from -0.1875 to 0.1875
- w_value: bfloat16 [1152, 256], P('fsdp'), may hold values from -0.1875 to 0.1875
- w_out: bfloat16 [1024, 1152], P('fsdp'), may hold values from -0.1875 to 0.1875
- w_gate: bfloat16 [1152, 6912], P('fsdp'), may hold values from -0.1875 to 0.1875
- w_up: bfloat16 [1152, 6912], P('fsdp'), may hold values from -0.1875 to 0.1875
- w_down: bfloat16 [6912, 1152], P('fsdp'), may hold values from -0.078125 to 0.078125
Outputs:
- layer_out: bfloat16 [4, 1024, 1152], P('fsdp', 'seq')
- grad_tokens: float32 [4, 1024, 1152], P('fsdp', 'seq')
- grad_attn_norm: float32 [1152], P(('seq', 'fsdp'))
- grad_q_norm: float32 [256], P(('seq', 'fsdp'))
- grad_k_norm: float32 [256], P(('seq', 'fsdp'))
- grad_post_attn_norm: float32 [1152], P(('seq', 'fsdp'))
- grad_ffn_norm: float32 [1152], P(('seq', 'fsdp'))
- grad_post_ffn_norm: float32 [1152], P(('seq', 'fsdp'))
- grad_w_query: float32 [1152, 1024], P(('seq', 'fsdp'))
- grad_w_key: float32 [1152, 256], P(('seq', 'fsdp'))
- grad_w_value: float32 [1152, 256], P(('seq', 'fsdp'))
- grad_w_out: float32 [1024, 1152], P(None, ('seq', 'fsdp'))
- grad_w_gate: float32 [1152, 6912], P(('seq', 'fsdp'))
- grad_w_up: float32 [1152, 6912], P(('seq', 'fsdp'))
- grad_w_down: float32 [6912, 1152], P(None, ('seq', 'fsdp'))
All inputs are finite; a program needn't handle non-finite values.
Results may differ from a plain program's by a relative error of at most 0.019.
Values may be sent and summed in bfloat16 or wider, within the bound.
A program may use at most 448 MiB of HBM per device.

v0:
```python
import jax
import jax.numpy as jnp
from jax import lax
from jax.sharding import PartitionSpec as P

HQ = 4
HD = 256
W = 512


epsilon = 1e-06


def passed_along(value, axis, steps):
    count = lax.axis_size(axis)
    leading, last = (max(0, -steps), min(count, count - steps))
    return lax.ppermute(value, axis, [(source, source + steps) for source in range(leading, last)])


def norm_forward(vector, gain_vec):
    factor = lax.rsqrt(jnp.mean(vector * vector, axis=-1, keepdims=True) + epsilon)
    normed = vector * factor
    return (normed * gain_vec, normed, factor)


def norm_backward(upstream, gain_vec, normed, factor):
    scaled = upstream * gain_vec
    grad_input = factor * (scaled - normed * jnp.mean(scaled * normed, axis=-1, keepdims=True))
    grad_gain = jnp.sum((upstream * normed).reshape(-1, normed.shape[-1]), axis=0)
    return (grad_input, grad_gain)


def rope_tables(position, head_width):
    half_width = head_width // 2
    frequency = 10000.0 ** (-(jnp.arange(half_width).astype(jnp.float32) * (2.0 / head_width)))
    angles = position.astype(jnp.float32)[:, None] * frequency[None, :]
    return (jnp.cos(angles), jnp.sin(angles))


def rotate(vector, cos_table, sin_table):
    half_width = vector.shape[-1] // 2
    lead_half = vector[..., :half_width]
    tail_half = vector[..., half_width:]
    return jnp.concatenate(
        [
            lead_half * cos_table - tail_half * sin_table,
            tail_half * cos_table + lead_half * sin_table,
        ],
        axis=-1,
    )


def unrotate(upstream, cos_table, sin_table):
    half_width = upstream.shape[-1] // 2
    lead_half = upstream[..., :half_width]
    tail_half = upstream[..., half_width:]
    return jnp.concatenate(
        [
            lead_half * cos_table + tail_half * sin_table,
            tail_half * cos_table - lead_half * sin_table,
        ],
        axis=-1,
    )


def window_mask(query_pos, key_pos):
    distance = query_pos[:, None] - key_pos[None, :]
    return (distance >= 0) & (distance < W) & (key_pos[None, :] >= 0)


def score_rows(query_bf, key_window, query_pos, key_pos):
    scores = jnp.einsum(
        "bhd,ld->hbl", query_bf, key_window, preferred_element_type=jnp.float32
    ) * HD ** (-0.5)
    return jnp.where(window_mask(query_pos, key_pos)[None], scores, -1e30)


def attend(query_bf, key_window, value_window, query_pos, key_pos):
    scores = score_rows(query_bf, key_window, query_pos, key_pos)
    row_peak = jnp.max(scores, axis=-1, keepdims=True)
    row_total = jnp.sum(jnp.exp(scores - row_peak), axis=-1, keepdims=True)
    log_total = row_peak + jnp.log(row_total)
    prob_bf = jnp.exp(scores - log_total).astype(jnp.bfloat16)
    mixed_rows = jnp.einsum(
        "hbl,ld->bhd", prob_bf, value_window, preferred_element_type=jnp.float32
    )
    return (mixed_rows, log_total[..., 0])


def attend_back(
    query_bf, key_window, value_window, query_pos, key_pos, mixed_rows, log_total, grad_mixed_bf
):
    scores = score_rows(query_bf, key_window, query_pos, key_pos)
    prob_rows = jnp.exp(scores - log_total[..., None])
    prob_bf = prob_rows.astype(jnp.bfloat16)
    grad_values = jnp.einsum(
        "hbl,bhd->ld", prob_bf, grad_mixed_bf, preferred_element_type=jnp.float32
    )
    grad_probs = jnp.einsum(
        "bhd,ld->hbl", grad_mixed_bf, value_window, preferred_element_type=jnp.float32
    )
    row_delta = jnp.sum(grad_mixed_bf.astype(jnp.float32) * mixed_rows, axis=-1)
    grad_scores_bf = (
        prob_rows * (grad_probs - jnp.transpose(row_delta)[:, :, None]) * HD ** (-0.5)
    ).astype(jnp.bfloat16)
    grad_queries = jnp.einsum(
        "hbl,ld->bhd", grad_scores_bf, key_window, preferred_element_type=jnp.float32
    )
    grad_keys = jnp.einsum(
        "hbl,bhd->ld", grad_scores_bf, query_bf, preferred_element_type=jnp.float32
    )
    return (grad_queries, grad_keys, grad_values)


def matmul(left_op, right_op):
    return jnp.dot(left_op, right_op, preferred_element_type=jnp.float32)


def contract_rows(left_op, right_op):
    return lax.dot_general(
        left_op, right_op, (((0,), (0,)), ((), ())), preferred_element_type=jnp.float32
    )


def contract_cols(left_op, right_op):
    return lax.dot_general(
        left_op, right_op, (((1,), (1,)), ((), ())), preferred_element_type=jnp.float32
    )


def on_device(
    tokens,
    cotangent,
    attn_norm,
    q_norm,
    k_norm,
    post_attn_norm,
    ffn_norm,
    post_ffn_norm,
    w_query,
    w_key,
    w_value,
    w_out,
    w_gate,
    w_up,
    w_down,
):
    block_rows = tokens.shape[1]
    halo_rows = min(block_rows, W)
    halo_count = W // halo_rows
    attn_set = (
        lax.all_gather(attn_norm, "fsdp", axis=0, tiled=True),
        lax.all_gather(q_norm, "fsdp", axis=0, tiled=True),
        lax.all_gather(k_norm, "fsdp", axis=0, tiled=True),
        lax.all_gather(post_attn_norm, "fsdp", axis=0, tiled=True),
        lax.all_gather(w_query, "fsdp", axis=0, tiled=True),
        lax.all_gather(w_key, "fsdp", axis=0, tiled=True),
        lax.all_gather(w_value, "fsdp", axis=0, tiled=True),
        lax.all_gather(w_out, "fsdp", axis=0, tiled=True),
    )
    ffn_set = (
        lax.all_gather(ffn_norm, "fsdp", axis=0, tiled=True),
        lax.all_gather(post_ffn_norm, "fsdp", axis=0, tiled=True),
        lax.all_gather(w_gate, "fsdp", axis=0, tiled=True),
        lax.all_gather(w_up, "fsdp", axis=0, tiled=True),
        lax.all_gather(w_down, "fsdp", axis=0, tiled=True),
    )
    gain_attn = attn_set[0].astype(jnp.float32)
    gain_query = attn_set[1].astype(jnp.float32)
    gain_key = attn_set[2].astype(jnp.float32)
    gain_post_attn = attn_set[3].astype(jnp.float32)
    gain_ffn = ffn_set[0].astype(jnp.float32)
    gain_post_ffn = ffn_set[1].astype(jnp.float32)
    base_row = lax.axis_index("seq") * block_rows
    query_pos = base_row + jnp.arange(block_rows, dtype=jnp.int32)
    key_pos = base_row - W + jnp.arange(W + block_rows, dtype=jnp.int32)
    cos_table, sin_table = rope_tables(query_pos, HD)
    residual = tokens[0].astype(jnp.float32)
    attn_scaled, attn_unit, attn_factor = norm_forward(residual, gain_attn)
    attn_in = attn_scaled.astype(jnp.bfloat16)
    query_raw = matmul(attn_in, attn_set[4]).reshape(block_rows, HQ, HD)
    key_raw = matmul(attn_in, attn_set[5])
    value_raw = matmul(attn_in, attn_set[6])
    query_scaled, query_unit, query_factor = norm_forward(query_raw, gain_query)
    key_scaled, key_unit, key_factor = norm_forward(key_raw, gain_key)
    query_bf = rotate(query_scaled, cos_table[:, None, :], sin_table[:, None, :]).astype(
        jnp.bfloat16
    )
    key_bf = rotate(key_scaled, cos_table, sin_table).astype(jnp.bfloat16)
    value_bf = value_raw.astype(jnp.bfloat16)
    key_parts = []
    value_parts = []
    for offset in range(halo_count, 0, -1):
        got_keys, got_values = passed_along((key_bf, value_bf), "seq", offset)
        key_parts.append(got_keys)
        value_parts.append(got_values)
    key_window = jnp.concatenate(key_parts + [key_bf], axis=0)
    value_window = jnp.concatenate(value_parts + [value_bf], axis=0)
    mixed_rows, log_total = attend(query_bf, key_window, value_window, query_pos, key_pos)
    mixed_bf = mixed_rows.reshape(block_rows, HQ * HD).astype(jnp.bfloat16)
    branch = matmul(mixed_bf, attn_set[7])
    branch_out, branch_unit, branch_factor = norm_forward(branch, gain_post_attn)
    hidden = residual + branch_out
    ffn_scaled, ffn_unit, ffn_factor = norm_forward(hidden, gain_ffn)
    ffn_in = ffn_scaled.astype(jnp.bfloat16)
    gate_pre = matmul(ffn_in, ffn_set[2])
    up_pre = matmul(ffn_in, ffn_set[3])
    gate_act = jax.nn.gelu(gate_pre, approximate=True)
    product_bf = (gate_act * up_pre).astype(jnp.bfloat16)
    down_pre = matmul(product_bf, ffn_set[4])
    down_out, down_unit, down_factor = norm_forward(down_pre, gain_post_ffn)
    layer_out = (hidden + down_out).astype(jnp.bfloat16)
    upstream = cotangent[0].astype(jnp.float32)
    grad_down, grad_post_ffn = norm_backward(upstream, gain_post_ffn, down_unit, down_factor)
    grad_down_bf = grad_down.astype(jnp.bfloat16)
    grad_product = contract_cols(grad_down_bf, ffn_set[4])
    grad_up_bf = (grad_product * gate_act).astype(jnp.bfloat16)
    unused_value, gelu_back = jax.vjp(
        lambda pre_act: jax.nn.gelu(pre_act, approximate=True), gate_pre
    )
    grad_gate_bf = gelu_back(grad_product * up_pre)[0].astype(jnp.bfloat16)
    grad_ffn_in = contract_cols(grad_gate_bf, ffn_set[2]) + contract_cols(grad_up_bf, ffn_set[3])
    grad_hidden_ffn, grad_ffn = norm_backward(grad_ffn_in, gain_ffn, ffn_unit, ffn_factor)
    grad_hidden = upstream + grad_hidden_ffn
    grad_branch, grad_post_attn = norm_backward(
        grad_hidden, gain_post_attn, branch_unit, branch_factor
    )
    grad_branch_bf = grad_branch.astype(jnp.bfloat16)
    grad_mixed_bf = (
        contract_cols(grad_branch_bf, attn_set[7]).astype(jnp.bfloat16).reshape(block_rows, HQ, HD)
    )
    grad_query_rot, grad_key_window, grad_value_window = attend_back(
        query_bf, key_window, value_window, query_pos, key_pos, mixed_rows, log_total, grad_mixed_bf
    )
    back_keys = jnp.zeros((halo_rows, HD), jnp.float32)
    back_values = jnp.zeros((halo_rows, HD), jnp.float32)
    for offset in range(halo_count, 0, -1):
        row_start = (halo_count - offset) * halo_rows
        piece_keys = grad_key_window[row_start : row_start + halo_rows]
        piece_values = grad_value_window[row_start : row_start + halo_rows]
        got_keys, got_values = (
            passed_along(piece_keys.astype(jnp.bfloat16), "seq", -offset).astype(piece_keys.dtype),
            passed_along(piece_values.astype(jnp.bfloat16), "seq", -offset).astype(
                piece_values.dtype
            ),
        )
        back_keys = back_keys + got_keys
        back_values = back_values + got_values
    own_keys = grad_key_window[W:]
    own_values = grad_value_window[W:]
    kept_rows = block_rows - halo_rows
    grad_key_rot = jnp.concatenate([own_keys[:kept_rows], own_keys + back_keys], axis=0)
    grad_value = jnp.concatenate([own_values[:kept_rows], own_values + back_values], axis=0)
    grad_query_raw, grad_q = norm_backward(
        unrotate(grad_query_rot, cos_table[:, None, :], sin_table[:, None, :]),
        gain_query,
        query_unit,
        query_factor,
    )
    grad_key_raw, grad_k = norm_backward(
        unrotate(grad_key_rot, cos_table, sin_table), gain_key, key_unit, key_factor
    )
    grad_query_bf = grad_query_raw.reshape(block_rows, HQ * HD).astype(jnp.bfloat16)
    grad_key_bf = grad_key_raw.astype(jnp.bfloat16)
    grad_value_bf = grad_value.astype(jnp.bfloat16)
    grad_attn_in = (
        contract_cols(grad_query_bf, attn_set[4])
        + contract_cols(grad_key_bf, attn_set[5])
        + contract_cols(grad_value_bf, attn_set[6])
    )
    grad_residual, grad_attn = norm_backward(grad_attn_in, gain_attn, attn_unit, attn_factor)
    grad_tokens = grad_hidden + grad_residual
    ffn_right = jnp.concatenate([grad_gate_bf, grad_up_bf], axis=1)
    attn_right = jnp.concatenate([grad_query_bf, grad_key_bf, grad_value_bf], axis=1)
    weight_sums = lax.psum_scatter(
        jnp.concatenate(
            [
                contract_rows(ffn_in, ffn_right),
                contract_rows(attn_in, attn_right),
                contract_rows(grad_down_bf, product_bf),
                contract_rows(grad_branch_bf, mixed_bf),
            ],
            axis=1,
        ),
        ("seq", "fsdp"),
        scatter_dimension=0,
        tiled=True,
    )
    gain_sums = (
        lax.psum_scatter(grad_attn, ("seq", "fsdp"), scatter_dimension=0, tiled=True),
        lax.psum_scatter(grad_q, ("seq", "fsdp"), scatter_dimension=0, tiled=True),
        lax.psum_scatter(grad_k, ("seq", "fsdp"), scatter_dimension=0, tiled=True),
        lax.psum_scatter(grad_post_attn, ("seq", "fsdp"), scatter_dimension=0, tiled=True),
        lax.psum_scatter(grad_ffn, ("seq", "fsdp"), scatter_dimension=0, tiled=True),
        lax.psum_scatter(grad_post_ffn, ("seq", "fsdp"), scatter_dimension=0, tiled=True),
    )
    ffn_width = grad_gate_bf.shape[1]
    query_width = grad_query_bf.shape[1]
    head_width = grad_key_bf.shape[1]
    edge_up = ffn_width + ffn_width
    edge_query = edge_up + query_width
    edge_key = edge_query + head_width
    edge_value = edge_key + head_width
    edge_down = edge_value + ffn_width
    edge_out = edge_down + query_width
    grad_w_gate = weight_sums[:, :ffn_width]
    grad_w_up = weight_sums[:, ffn_width:edge_up]
    grad_w_query = weight_sums[:, edge_up:edge_query]
    grad_w_key = weight_sums[:, edge_query:edge_key]
    grad_w_value = weight_sums[:, edge_key:edge_value]
    grad_w_down = jnp.transpose(weight_sums[:, edge_value:edge_down])
    grad_w_out = jnp.transpose(weight_sums[:, edge_down:edge_out])
    return (
        layer_out[None],
        grad_tokens[None],
        gain_sums[0],
        gain_sums[1],
        gain_sums[2],
        gain_sums[3],
        gain_sums[4],
        gain_sums[5],
        grad_w_query,
        grad_w_key,
        grad_w_value,
        grad_w_out,
        grad_w_gate,
        grad_w_up,
        grad_w_down,
    )


def solution(mesh):
    in_specs = (
        P("fsdp", "seq", None),
        P("fsdp", "seq", None),
        P("fsdp"),
        P("fsdp"),
        P("fsdp"),
        P("fsdp"),
        P("fsdp"),
        P("fsdp"),
        P("fsdp", None),
        P("fsdp", None),
        P("fsdp", None),
        P("fsdp", None),
        P("fsdp", None),
        P("fsdp", None),
        P("fsdp", None),
    )
    out_specs = (
        P("fsdp", "seq", None),
        P("fsdp", "seq", None),
        P(("seq", "fsdp")),
        P(("seq", "fsdp")),
        P(("seq", "fsdp")),
        P(("seq", "fsdp")),
        P(("seq", "fsdp")),
        P(("seq", "fsdp")),
        P(("seq", "fsdp"), None),
        P(("seq", "fsdp"), None),
        P(("seq", "fsdp"), None),
        P(None, ("seq", "fsdp")),
        P(("seq", "fsdp"), None),
        P(("seq", "fsdp"), None),
        P(None, ("seq", "fsdp")),
    )
    return jax.shard_map(
        on_device, mesh=mesh, in_specs=in_specs, out_specs=out_specs, check_vma=False
    )
```

profile of v0, /device:TPU:0, one launch (start us, length us, event | category | flops | bytes accessed | tf_op | source)
XLA Modules:
  0.0 2094.1 jit_solution(4743335451483456513)
XLA Ops:
  14.1 13.8 all-reduce.14
  28.2 10.8 all_gather.41
  40.7 4.4 collective-permute-start.4
  45.0 4.3 collective-permute-start.5
  50.7 3.1 collective-permute-start.7
  53.8 11.0 all_gather.40
  68.2 2.3 collective-permute-start.1
  73.1 3.3 collective-permute-start.3
  81.4 3.3 copy.61
  87.7 2.2 fusion.90
  89.9 2.4 multiply_reduce_fusion.6
  93.6 76.8 %all-gather.10.cloned.1.call-done = bf16[1152,6912]{1,0:T(8,128)(2,1)} async-done(((bf16[288,6912]{1,0:T(8,128)(2,1)}), bf16[1152,6912]{1,0:T(8,128)(2,1)}) %all-gather.10.cloned.1.call-update) | async-done | bytes 15925264 | tf_op jit(solution)/shard_map/all_gather | solution.py:164
  170.4 9.8 fusion.93
  180.3 92.7 %all-gather.12.cloned.1.call-done = bf16[1152,6912]{1,0:T(8,128)(2,1)} async-done(((bf16[288,6912]{1,0:T(8,128)(2,1)}), bf16[1152,6912]{1,0:T(8,128)(2,1)}) %all-gather.12.cloned.1.call-update) | async-done | bytes 15925264 | tf_op jit(solution)/shard_map/all_gather | solution.py:165
  272.9 11.4 multiply_convert_fusion.1
  284.3 91.1 %all-gather.14.cloned.1.call-done = bf16[6912,1152]{1,0:T(8,128)(2,1)} async-done(((bf16[1728,1152]{1,0:T(8,128)(2,1)}), bf16[6912,1152]{1,0:T(8,128)(2,1)}) %all-gather.14.cloned.1.call-update) | async-done | bytes 15925264 | tf_op jit(solution)/shard_map/all_gather | solution.py:166
  375.4 8.2 multiply_reduce_fusion.4
  385.4 10.8 multiply_convert_fusion
  396.3 11.9 fusion.94
  408.2 12.1 multiply_reduce_fusion
  429.8 2.2 convolution_bitcast_fusion.3
  434.6 3.0 fusion.97
  437.6 12.8 fusion.96
  450.5 24.4 %fusion.7 = f32[1152,13824]{1,0:T(8,128)} fusion(bf16[128,1152]{1,0:T(8,128)(2,1)S(1)} %copy-done.14, bf16[128,6912]{1,0:T(8,128)(2,1)S(1)} %copy-done.10, bf16[128,6912]{1,0:T(8,128)(2,1)} %get-tuple-element.50), kind=kOutput, calls=%fused_computation.10 | convolution fusion | flops 4083941376 | bytes 67534848 | tf_op jit(solution)/shard_map/dot_general | solution.py:120
  488.7 4.2 collective-permute-done.8
  495.0 5.9 collective-permute-done.12
  504.0 74.0 %pad_maximum_fusion = f32[1152,23296]{1,0:T(8,128)} fusion(f32[1152,1024]{1,0:T(8,128)S(1)} %bitcast.143, f32[1152,6912]{1,0:T(8,128)} %fusion.96, f32[1152,1536]{1,0:T(8,128)S(1)} %fusion.41, f32[1152,13824]{1,0:T(8,128)} %fusion.7), kind=kLoop, calls=%fused_computation | loop fusion | flops 80510976 | bytes 214695936 | tf_op jit(solution)/shard_map/concatenate | solution.py:276
  579.7 2.0 fusion.95
  584.6 39.1 %all-reduce.13 = (f32[1152]{0:T(1024)S(1)}, f32[256]{0:T(256)S(1)}, f32[256]{0:T(256)S(1)}, f32[1152]{0:T(1024)S(1)}, f32[1152]{0:T(1024)S(1)}, /*index=5*/f32[1152]{0:T(1024)S(1)}) all-reduce(f32[1152]{0:T(1024)S(1)} %get-tuple-element.23, f32[256]{0:T(256)S(1)} %get-tuple-element.19, ...), channel_id=2, replica_groups=mesh['seq'=8,'fsdp'=4] {'seq','fsdp'}, use_global_device_ids=true, to_apply=%region_16.17.clone | all-reduce | flops 5120 | bytes 40960
  628.3 1450.4 %all-reduce.17.cloned.1.call-done = f32[1152,23296]{1,0:T(8,128)} async-done(((f32[1152,23296]{1,0:T(8,128)}), f32[1152,23296]{1,0:T(8,128)}) %all-reduce.17.cloned.1.call-update) | async-done | bytes 107347984
  2078.7 1.9 dynamic-slice_bitcast_fusion.1
  2082.3 4.5 dynamic-slice_bitcast_fusion
  (264 shorter events, 67.1 us)
Async XLA Ops:
  7.2 74.2 %all-gather.6.cloned.1.call-start = ((), (), s32[]{:S(2)}) async-start(), calls=%async_computation | async-start | bytes 2949120 | tf_op jit(solution)/shard_map/all_gather | solution.py:156
  7.9 82.0 %all-gather.8.cloned.1.call-start = ((), (), s32[]{:S(2)}) async-start(), calls=%async_computation.1 | async-start | bytes 2949120 | tf_op jit(solution)/shard_map/all_gather | solution.py:159
  8.7 161.8 %all-gather.10.cloned.1.call-start = ((), (), s32[]{:S(2)}) async-start(), calls=%async_computation.2 | async-start | bytes 19906560 | tf_op jit(solution)/shard_map/all_gather | solution.py:164
  9.5 263.4 %all-gather.12.cloned.1.call-start = ((), (), s32[]{:S(2)}) async-start(), calls=%async_computation.3 | async-start | bytes 19906560 | tf_op jit(solution)/shard_map/all_gather | solution.py:165
  10.1 43.7 %copy-start.38 = (bf16[288,256]{1,0:T(8,128)(2,1)S(1)}, bf16[288,256]{1,0:T(8,128)(2,1)}, u32[]{:S(2)}) copy-start(bf16[288,256]{1,0:T(8,128)(2,1)} %param.25) | copy-start | bytes 442372
  10.1 365.3 %all-gather.14.cloned.1.call-start = ((), (), s32[]{:S(2)}) async-start(), calls=%async_computation.4 | async-start | bytes 19906560 | tf_op jit(solution)/shard_map/all_gather | solution.py:166
  10.7 2068.1 %all-reduce.17.cloned.1.call-start = ((), (), s32[]{:S(2)}) async-start(), calls=%async_computation.5 | async-start | bytes 214695936
  28.0 40.1 %copy-start.43 = (f32[256]{0:T(256)}, f32[256]{0:T(256)S(1)}, u32[]{:S(2)}) copy-start(f32[256]{0:T(256)S(1)} %convert_element_type.149) | copy-start | bytes 3076
  39.8 44.9 %copy-start.41 = (f32[128]{0:T(128)}, f32[128]{0:T(128)S(1)}, u32[]{:S(2)}) copy-start(f32[128]{0:T(128)S(1)} %add_rsqrt_fusion.5) | copy-start | bytes 1540
  40.6 45.3 %copy-start.29 = (f32[128,128]{1,0:T(8,128)}, f32[128,128]{1,0:T(8,128)S(1)}, u32[]{:S(2)}) copy-start(f32[128,128]{1,0:T(8,128)S(1)} %get-tuple-element.69) | copy-start | bytes 196612
  40.6 45.3 %copy-start.31 = (f32[128,128]{1,0:T(8,128)}, f32[128,128]{1,0:T(8,128)S(1)}, u32[]{:S(2)}) copy-start(f32[128,128]{1,0:T(8,128)S(1)} %get-tuple-element.70) | copy-start | bytes 196612
  40.7 27.5 %collective-permute-start.4 = (bf16[128,256]{1,0:T(8,128)(2,1)S(1)}, bf16[128,256]{1,0:T(8,128)(2,1)S(1)}, u32[]{:S(2)}, u32[]{:S(2)}) collective-permute-start(bf16[128,256]{1,0:T(8,128)(2,1)S(1)} %pad_maximum_fusion.6), channel_id=1, source_target_pairs={{0,16},{4,20},{8,24},{12,28},{1,17},{5,21},{9,25},{13,29},{2,18},{... | collective-permute-start | bytes 196616 | tf_op jit(solution)/shard_map/ppermute | solution.py:17
  45.0 26.1 %collective-permute-start.5 = (bf16[128,256]{1,0:T(8,128)(2,1)S(1)}, bf16[128,256]{1,0:T(8,128)(2,1)S(1)}, u32[]{:S(2)}, u32[]{:S(2)}) collective-permute-start(bf16[128,256]{1,0:T(8,128)(2,1)S(1)} %pad_maximum_fusion.6), channel_id=1, source_target_pairs={{0,12},{4,16},{8,20},{12,24},{16,28},{1,13},{5,17},{9,21},{13,25},... | collective-permute-start | bytes 196616 | tf_op jit(solution)/shard_map/ppermute | solution.py:17
  49.4 23.7 %collective-permute-start.6 = (bf16[128,256]{1,0:T(8,128)(2,1)S(1)}, bf16[128,256]{1,0:T(8,128)(2,1)S(1)}, u32[]{:S(2)}, u32[]{:S(2)}) collective-permute-start(bf16[128,256]{1,0:T(8,128)(2,1)S(1)} %pad_maximum_fusion.6), channel_id=1, source_target_pairs={{0,8},{4,12},{8,16},{12,20},{16,24},{20,28},{1,9},{5,13},{9,17},{1... | collective-permute-start | bytes 196616 | tf_op jit(solution)/shard_map/ppermute | solution.py:17
  50.7 26.3 %collective-permute-start.7 = (bf16[128,256]{1,0:T(8,128)(2,1)S(1)}, bf16[128,256]{1,0:T(8,128)(2,1)S(1)}, u32[]{:S(2)}, u32[]{:S(2)}) collective-permute-start(bf16[128,256]{1,0:T(8,128)(2,1)S(1)} %pad_maximum_fusion.6), channel_id=1, source_target_pairs={{0,4},{4,8},{8,12},{12,16},{16,20},{20,24},{24,28},{1,5},{5,9},{9,... | collective-permute-start | bytes 196616 | tf_op jit(solution)/shard_map/ppermute | solution.py:17
  65.9 12.3 collective-permute-start
  68.2 10.6 collective-permute-start.1
  71.1 8.4 collective-permute-start.2
  73.1 7.1 collective-permute-start.3
  92.3 87.9 %copy-start.6 = (f32[128,1152]{1,0:T(8,128)}, f32[128,1152]{1,0:T(8,128)S(1)}, u32[]{:S(2)}) copy-start(f32[128,1152]{1,0:T(8,128)S(1)} %get-tuple-element.82) | copy-start | bytes 1769476
  92.3 87.9 %copy-start.47 = (f32[128]{0:T(128)}, f32[128]{0:T(128)S(1)}, u32[]{:S(2)}) copy-start(f32[128]{0:T(128)S(1)} %add_rsqrt_fusion.3) | copy-start | bytes 1540
  92.7 315.5 %copy-start.51 = (f32[128]{0:T(128)}, f32[128]{0:T(128)S(1)}, u32[]{:S(2)}) copy-start(f32[128]{0:T(128)S(1)} %add_rsqrt_fusion.2) | copy-start | bytes 1540
  93.6 86.7 %copy-start.13 = (bf16[128,1152]{1,0:T(8,128)(2,1)}, bf16[128,1152]{1,0:T(8,128)(2,1)S(1)}, u32[]{:S(2)}) copy-start(bf16[128,1152]{1,0:T(8,128)(2,1)S(1)} %multiply_convert_fusion.3) | copy-start | bytes 884740
  475.9 6.8 collective-permute-start.11
  477.2 7.7 collective-permute-start.10
  478.5 8.9 collective-permute-start.9
  479.8 13.1 collective-permute-start.8
  481.3 13.3 collective-permute-start.15
  482.6 12.0 collective-permute-start.14
  484.9 10.1 collective-permute-start.13
  487.4 13.5 collective-permute-start.12
  579.7 47.6 %copy-start.12 = (f32[128,1152]{1,0:T(8,128)S(1)}, f32[128,1152]{1,0:T(8,128)}, u32[]{:S(2)}) copy-start(f32[128,1152]{1,0:T(8,128)} %copy-done.11) | copy-start | bytes 1769476
  (55 other events, 601.5 us)
Sparse Core Ops, SparseCore 0:
  9.5 30.2 all-gather.5
  41.4 27.1 all-gather.7
  70.2 100.1 all-gather.9
  171.8 101.0 all-gather.11
  274.3 101.0 all-gather.13
  578.2 1500.5 all-reduce.16
where the time goes:
time: 2100 us; the launch traced here: 2090 us
  waiting for transfers between devices  1730 us (82%)
  matrix products  126 us (6%)
  other arithmetic  85.9 us (4%)
  blocking collectives  74.7 us (4%)
  local copies, waits for them, and re-layouts  31.9 us (2%)
  starting transfers between devices  31.8 us (2%)
    unnamed x7, waiting for transfers between devices  1450 us
    all_gather x1, waiting for transfers between devices, on_device(): lax.all_gather(w_up, 'fsdp', axis=0, tiled=True)  92.7 us
    all_gather x1, waiting for transfers between devices, on_device(): lax.all_gather(w_down, 'fsdp', axis=0, tiled=True)  91.1 us
    all_gather x1, waiting for transfers between devices, on_device(): lax.all_gather(w_gate, 'fsdp', axis=0, tiled=True)  76.8 us
    concatenate x1, other arithmetic, on_device(): jnp.concatenate([contract_rows(ffn_in, ffn_right), contract_rows(attn_in,...  74 us
    unnamed x2, blocking collectives  53 us
  transfers between devices with their start and end apart: 22, of which 9 were waited for; matrix products, arithmetic and copies ran while one was open for 3% of the time, Pallas kernels for 0%

commit v1 on v0

--- a/solution.py
+++ b/solution.py
@@ -126,6 +126,22 @@
     return lax.dot_general(
         left_op, right_op, (((1,), (1,)), ((), ())), preferred_element_type=jnp.float32
     )
+
+
+def row_sums(partial):
+    return lax.psum_scatter(
+        partial.astype(jnp.bfloat16), "seq", scatter_dimension=0, tiled=True
+    ).astype(jnp.float32)
+
+
+def placed(rows, owned, padded, seq_size, fsdp_size):
+    slot = jnp.arange(seq_size * fsdp_size * padded)
+    block = slot // padded
+    inner = slot % padded
+    owner = (block % seq_size) * fsdp_size + block // seq_size
+    source = jnp.where(inner < owned, owner * owned + inner, -1)
+    pick = (jnp.arange(rows.shape[1])[:, None] == source[None, :]).astype(jnp.bfloat16)
+    return matmul(rows, pick).astype(jnp.bfloat16)
 
 
 def on_device(
@@ -148,29 +164,46 @@
     block_rows = tokens.shape[1]
     halo_rows = min(block_rows, W)
     halo_count = W // halo_rows
-    attn_set = (
-        lax.all_gather(attn_norm, "fsdp", axis=0, tiled=True),
-        lax.all_gather(q_norm, "fsdp", axis=0, tiled=True),
-        lax.all_gather(k_norm, "fsdp", axis=0, tiled=True),
-        lax.all_gather(post_attn_norm, "fsdp", axis=0, tiled=True),
-        lax.all_gather(w_query, "fsdp", axis=0, tiled=True),
-        lax.all_gather(w_key, "fsdp", axis=0, tiled=True),
-        lax.all_gather(w_value, "fsdp", axis=0, tiled=True),
-        lax.all_gather(w_out, "fsdp", axis=0, tiled=True),
-    )
-    ffn_set = (
-        lax.all_gather(ffn_norm, "fsdp", axis=0, tiled=True),
-        lax.all_gather(post_ffn_norm, "fsdp", axis=0, tiled=True),
-        lax.all_gather(w_gate, "fsdp", axis=0, tiled=True),
-        lax.all_gather(w_up, "fsdp", axis=0, tiled=True),
-        lax.all_gather(w_down, "fsdp", axis=0, tiled=True),
-    )
-    gain_attn = attn_set[0].astype(jnp.float32)
-    gain_query = attn_set[1].astype(jnp.float32)
-    gain_key = attn_set[2].astype(jnp.float32)
-    gain_post_attn = attn_set[3].astype(jnp.float32)
-    gain_ffn = ffn_set[0].astype(jnp.float32)
-    gain_post_ffn = ffn_set[1].astype(jnp.float32)
+    seq_size = lax.axis_size("seq")
+    fsdp_size = lax.axis_size("fsdp")
+    owners = seq_size * fsdp_size
+    seq_index = lax.axis_index("seq")
+    width = tokens.shape[2]
+    qkv_local = jnp.concatenate([w_query, w_key, w_value], axis=1)
+    gains_local = (attn_norm, post_attn_norm, ffn_norm, post_ffn_norm, q_norm, k_norm)
+    gain_row = jnp.concatenate(gains_local)
+    gain_rows = jnp.pad(gain_row[None], ((0, 7), (0, qkv_local.shape[1] - gain_row.shape[0])))
+    packed = lax.all_gather(jnp.concatenate([qkv_local, gain_rows], axis=0), "fsdp", axis=0)
+    local_width = qkv_local.shape[0]
+    w_qkv = packed[:, :local_width].reshape(width, -1)
+    gain_all = packed[:, local_width].astype(jnp.float32)
+    gains = []
+    edge = 0
+    for part in gains_local:
+        gains.append(gain_all[:, edge : edge + part.shape[0]].reshape(-1))
+        edge += part.shape[0]
+    gain_attn, gain_post_attn, gain_ffn, gain_post_ffn, gain_query, gain_key = gains
+    w_out_full = lax.all_gather(w_out, "fsdp", axis=0, tiled=True)
+    ffn_block = w_down.shape[0]
+    piece = ffn_block // seq_size
+    slice_width = piece * fsdp_size
+
+    def hidden_slice(weight):
+        return jnp.concatenate(
+            [
+                lax.dynamic_slice_in_dim(weight, block * ffn_block + seq_index * piece, piece, 1)
+                for block in range(fsdp_size)
+            ],
+            axis=1,
+        )
+
+    gate_up_local = jnp.stack([hidden_slice(w_gate), hidden_slice(w_up)])
+    gate_up = lax.all_gather(gate_up_local, "fsdp", axis=0)
+    w_gate_part = gate_up[:, 0].reshape(width, slice_width)
+    w_up_part = gate_up[:, 1].reshape(width, slice_width)
+    w_down_part = lax.all_gather(
+        lax.dynamic_slice_in_dim(w_down, seq_index * piece, piece, 0), "fsdp", axis=0, tiled=True
+    )
     base_row = lax.axis_index("seq") * block_rows
     query_pos = base_row + jnp.arange(block_rows, dtype=jnp.int32)
     key_pos = base_row - W + jnp.arange(W + block_rows, dtype=jnp.int32)
@@ -178,9 +211,11 @@
     residual = tokens[0].astype(jnp.float32)
     attn_scaled, attn_unit, attn_factor = norm_forward(residual, gain_attn)
     attn_in = attn_scaled.astype(jnp.bfloat16)
-    query_raw = matmul(attn_in, attn_set[4]).reshape(block_rows, HQ, HD)
-    key_raw = matmul(attn_in, attn_set[5])
-    value_raw = matmul(attn_in, attn_set[6])
+    query_width = HQ * HD
+    qkv_raw = matmul(attn_in, w_qkv)
+    query_raw = qkv_raw[:, :query_width].reshape(block_rows, HQ, HD)
+    key_raw = qkv_raw[:, query_width : query_width + HD]
+    value_raw = qkv_raw[:, query_width + HD :]
     query_scaled, query_unit, query_factor = norm_forward(query_raw, gain_query)
     key_scaled, key_unit, key_factor = norm_forward(key_raw, gain_key)
     query_bf = rotate(query_scaled, cos_table[:, None, :], sin_table[:, None, :]).astype(
@@ -188,38 +223,41 @@
     )
     key_bf = rotate(key_scaled, cos_table, sin_table).astype(jnp.bfloat16)
     value_bf = value_raw.astype(jnp.bfloat16)
-    key_parts = []
-    value_parts = []
-    for offset in range(halo_count, 0, -1):
-        got_keys, got_values = passed_along((key_bf, value_bf), "seq", offset)
-        key_parts.append(got_keys)
-        value_parts.append(got_values)
-    key_window = jnp.concatenate(key_parts + [key_bf], axis=0)
-    value_window = jnp.concatenate(value_parts + [value_bf], axis=0)
+    both_bf = jnp.concatenate([key_bf, value_bf], axis=1)
+    both_parts = [passed_along(both_bf, "seq", offset) for offset in range(halo_count, 0, -1)]
+    both_window = jnp.concatenate(both_parts + [both_bf], axis=0)
+    key_window = both_window[:, :HD]
+    value_window = both_window[:, HD:]
     mixed_rows, log_total = attend(query_bf, key_window, value_window, query_pos, key_pos)
     mixed_bf = mixed_rows.reshape(block_rows, HQ * HD).astype(jnp.bfloat16)
-    branch = matmul(mixed_bf, attn_set[7])
+    branch = matmul(mixed_bf, w_out_full)
     branch_out, branch_unit, branch_factor = norm_forward(branch, gain_post_attn)
     hidden = residual + branch_out
     ffn_scaled, ffn_unit, ffn_factor = norm_forward(hidden, gain_ffn)
-    ffn_in = ffn_scaled.astype(jnp.bfloat16)
-    gate_pre = matmul(ffn_in, ffn_set[2])
-    up_pre = matmul(ffn_in, ffn_set[3])
+    ffn_in = lax.all_gather(ffn_scaled.astype(jnp.bfloat16), "seq", axis=0, tiled=True)
+    gate_pre = matmul(ffn_in, w_gate_part)
+    up_pre = matmul(ffn_in, w_up_part)
     gate_act = jax.nn.gelu(gate_pre, approximate=True)
     product_bf = (gate_act * up_pre).astype(jnp.bfloat16)
-    down_pre = matmul(product_bf, ffn_set[4])
+    down_pre = row_sums(matmul(product_bf, w_down_part))
     down_out, down_unit, down_factor = norm_forward(down_pre, gain_post_ffn)
     layer_out = (hidden + down_out).astype(jnp.bfloat16)
     upstream = cotangent[0].astype(jnp.float32)
     grad_down, grad_post_ffn = norm_backward(upstream, gain_post_ffn, down_unit, down_factor)
-    grad_down_bf = grad_down.astype(jnp.bfloat16)
-    grad_product = contract_cols(grad_down_bf, ffn_set[4])
+    grad_down_bf = lax.all_gather(grad_down.astype(jnp.bfloat16), "seq", axis=0, tiled=True)
+    grad_product = contract_cols(grad_down_bf, w_down_part)
     grad_up_bf = (grad_product * gate_act).astype(jnp.bfloat16)
     unused_value, gelu_back = jax.vjp(
         lambda pre_act: jax.nn.gelu(pre_act, approximate=True), gate_pre
     )
     grad_gate_bf = gelu_back(grad_product * up_pre)[0].astype(jnp.bfloat16)
-    grad_ffn_in = contract_cols(grad_gate_bf, ffn_set[2]) + contract_cols(grad_up_bf, ffn_set[3])
+    grad_ffn_part = (
+        contract_cols(grad_gate_bf, w_gate_part) + contract_cols(grad_up_bf, w_up_part)
+    ).astype(jnp.bfloat16)
+    grad_ffn_part, grad_gate_bf, grad_up_bf, product_bf = lax.optimization_barrier(
+        (grad_ffn_part, grad_gate_bf, grad_up_bf, product_bf)
+    )
+    grad_ffn_in = row_sums(grad_ffn_part)
     grad_hidden_ffn, grad_ffn = norm_backward(grad_ffn_in, gain_ffn, ffn_unit, ffn_factor)
     grad_hidden = upstream + grad_hidden_ffn
     grad_branch, grad_post_attn = norm_backward(
@@ -227,25 +265,19 @@
     )
     grad_branch_bf = grad_branch.astype(jnp.bfloat16)
     grad_mixed_bf = (
-        contract_cols(grad_branch_bf, attn_set[7]).astype(jnp.bfloat16).reshape(block_rows, HQ, HD)
+        contract_cols(grad_branch_bf, w_out_full).astype(jnp.bfloat16).reshape(block_rows, HQ, HD)
     )
     grad_query_rot, grad_key_window, grad_value_window = attend_back(
         query_bf, key_window, value_window, query_pos, key_pos, mixed_rows, log_total, grad_mixed_bf
     )
-    back_keys = jnp.zeros((halo_rows, HD), jnp.float32)
-    back_values = jnp.zeros((halo_rows, HD), jnp.float32)
+    back_both = jnp.zeros((halo_rows, 2 * HD), jnp.float32)
+    both_halo = jnp.concatenate([grad_key_window[:W], grad_value_window[:W]], axis=1)
     for offset in range(halo_count, 0, -1):
         row_start = (halo_count - offset) * halo_rows
-        piece_keys = grad_key_window[row_start : row_start + halo_rows]
-        piece_values = grad_value_window[row_start : row_start + halo_rows]
-        got_keys, got_values = (
-            passed_along(piece_keys.astype(jnp.bfloat16), "seq", -offset).astype(piece_keys.dtype),
-            passed_along(piece_values.astype(jnp.bfloat16), "seq", -offset).astype(
-                piece_values.dtype
-            ),
-        )
-        back_keys = back_keys + got_keys
-        back_values = back_values + got_values
+        piece_both = both_halo[row_start : row_start + halo_rows].astype(jnp.bfloat16)
+        back_both = back_both + passed_along(piece_both, "seq", -offset).astype(jnp.float32)
+    back_keys = back_both[:, :HD]
+    back_values = back_both[:, HD:]
     own_keys = grad_key_window[W:]
     own_values = grad_value_window[W:]
     kept_rows = block_rows - halo_rows
@@ -263,53 +295,89 @@
     grad_query_bf = grad_query_raw.reshape(block_rows, HQ * HD).astype(jnp.bfloat16)
     grad_key_bf = grad_key_raw.astype(jnp.bfloat16)
     grad_value_bf = grad_value.astype(jnp.bfloat16)
-    grad_attn_in = (
-        contract_cols(grad_query_bf, attn_set[4])
-        + contract_cols(grad_key_bf, attn_set[5])
-        + contract_cols(grad_value_bf, attn_set[6])
-    )
+    attn_right = jnp.concatenate([grad_query_bf, grad_key_bf, grad_value_bf], axis=1)
+    grad_attn_in = contract_cols(attn_right, w_qkv)
     grad_residual, grad_attn = norm_backward(grad_attn_in, gain_attn, attn_unit, attn_factor)
     grad_tokens = grad_hidden + grad_residual
-    ffn_right = jnp.concatenate([grad_gate_bf, grad_up_bf], axis=1)
-    attn_right = jnp.concatenate([grad_query_bf, grad_key_bf, grad_value_bf], axis=1)
-    weight_sums = lax.psum_scatter(
-        jnp.concatenate(
-            [
-                contract_rows(ffn_in, ffn_right),
-                contract_rows(attn_in, attn_right),
-                contract_rows(grad_down_bf, product_bf),
-                contract_rows(grad_branch_bf, mixed_bf),
-            ],
-            axis=1,
-        ),
-        ("seq", "fsdp"),
+    owned = width // owners
+    padded = -(-(owned + 1) // 8) * 8
+    ffn_left = placed(ffn_in, owned, padded, seq_size, fsdp_size)
+    down_left = placed(grad_down_bf, owned, padded, seq_size, fsdp_size)
+    ffn_sums = jnp.stack(
+        [
+            contract_rows(left, right)
+            .astype(jnp.bfloat16)
+            .reshape(fsdp_size, seq_size * padded, slice_width)
+            for left, right in (
+                (ffn_left, grad_gate_bf),
+                (ffn_left, grad_up_bf),
+                (down_left, product_bf),
+            )
+        ],
+        axis=1,
+    )
+    ffn_sums = ffn_sums.reshape(-1, slice_width)
+    ffn_sums = lax.psum_scatter(ffn_sums, "fsdp", scatter_dimension=0, tiled=True)
+    ffn_sums = lax.all_to_all(
+        ffn_sums.reshape(3, seq_size, padded, slice_width), "seq", 1, 1, tiled=True
+    )
+    ffn_sums = (
+        ffn_sums[:, :, :owned]
+        .reshape(3, seq_size, owned, fsdp_size, piece)
+        .transpose(0, 2, 3, 1, 4)
+        .reshape(3, owned, fsdp_size * ffn_block)
+        .astype(jnp.float32)
+    )
+    gain_grads = (grad_attn, grad_post_attn, grad_ffn, grad_post_ffn, grad_q, grad_k)
+    gain_right = jnp.concatenate([part.reshape(owners, -1) for part in gain_grads], axis=1)
+    attn_width = attn_right.shape[1]
+    total_width = attn_width + query_width
+    owner = jnp.arange(owners)
+    owner_slot = ((owner % fsdp_size) * seq_size + owner // fsdp_size) * padded + owned
+    gain_left = (jnp.arange(owners * padded)[None, :] == owner_slot[:, None]).astype(jnp.bfloat16)
+    sum_left = jnp.concatenate(
+        [
+            placed(attn_in, owned, padded, seq_size, fsdp_size),
+            placed(grad_branch_bf, owned, padded, seq_size, fsdp_size),
+            gain_left,
+        ],
+        axis=0,
+    )
+    sum_right = jnp.concatenate(
+        [
+            jnp.pad(attn_right, ((0, 0), (0, query_width))),
+            jnp.pad(mixed_bf, ((0, 0), (attn_width, 0))),
+            jnp.pad(
+                gain_right.astype(jnp.bfloat16),
+                ((0, 0), (0, total_width - gain_right.shape[1])),
+            ),
+        ],
+        axis=0,
+    )
+    attn_sums = lax.psum_scatter(
+        contract_rows(sum_left, sum_right).astype(jnp.bfloat16),
+        "fsdp",
         scatter_dimension=0,
         tiled=True,
     )
-    gain_sums = (
-        lax.psum_scatter(grad_attn, ("seq", "fsdp"), scatter_dimension=0, tiled=True),
-        lax.psum_scatter(grad_q, ("seq", "fsdp"), scatter_dimension=0, tiled=True),
-        lax.psum_scatter(grad_k, ("seq", "fsdp"), scatter_dimension=0, tiled=True),
-        lax.psum_scatter(grad_post_attn, ("seq", "fsdp"), scatter_dimension=0, tiled=True),
-        lax.psum_scatter(grad_ffn, ("seq", "fsdp"), scatter_dimension=0, tiled=True),
-        lax.psum_scatter(grad_post_ffn, ("seq", "fsdp"), scatter_dimension=0, tiled=True),
-    )
-    ffn_width = grad_gate_bf.shape[1]
-    query_width = grad_query_bf.shape[1]
-    head_width = grad_key_bf.shape[1]
-    edge_up = ffn_width + ffn_width
-    edge_query = edge_up + query_width
-    edge_key = edge_query + head_width
-    edge_value = edge_key + head_width
-    edge_down = edge_value + ffn_width
-    edge_out = edge_down + query_width
-    grad_w_gate = weight_sums[:, :ffn_width]
-    grad_w_up = weight_sums[:, ffn_width:edge_up]
-    grad_w_query = weight_sums[:, edge_up:edge_query]
-    grad_w_key = weight_sums[:, edge_query:edge_key]
-    grad_w_value = weight_sums[:, edge_key:edge_value]
-    grad_w_down = jnp.transpose(weight_sums[:, edge_value:edge_down])
-    grad_w_out = jnp.transpose(weight_sums[:, edge_down:edge_out])
+    attn_sums = lax.psum_scatter(attn_sums, "seq", scatter_dimension=0, tiled=True).astype(
+        jnp.float32
+    )
+    gain_sums = []
+    edge = 0
+    for part in gain_grads:
+        count = part.shape[0] // owners
+        gain_sums.append(attn_sums[owned, edge : edge + count])
+        edge += count
+    grad_attn, grad_post_attn, grad_ffn, grad_post_ffn, grad_q, grad_k = gain_sums
+    gain_sums = (grad_attn, grad_q, grad_k, grad_post_attn, grad_ffn, grad_post_ffn)
+    grad_w_gate = ffn_sums[0]
+    grad_w_up = ffn_sums[1]
+    grad_w_down = jnp.transpose(ffn_sums[2])
+    grad_w_query = attn_sums[:owned, :query_width]
+    grad_w_key = attn_sums[:owned, query_width : query_width + HD]
+    grad_w_value = attn_sums[:owned, query_width + HD : attn_width]
+    grad_w_out = jnp.transpose(attn_sums[:owned, attn_width:])
     return (
         layer_out[None],
         grad_tokens[None],

time: 2100 us -> 619 us (0.29)
  waiting for transfers between devices: 1730 us -> 382 us
  blocking collectives: 74.7 us -> 0 us
  other arithmetic: 85.9 us -> 32 us
  matrix products: 126 us -> 83.9 us
  local copies, waits for them, and re-layouts: 31.9 us -> 73.8 us
    unnamed x7 -> x11, waiting for transfers between devices: 1450 us -> 0.86 us
    reduce_scatter x0 -> x5, waiting for transfers between devices: none -> 210 us  [the longest x2 79.5 us: row_sums(): lax.psum_scatter(partial.astype(jnp.bfloat16), 'seq', scatter_dimension=0...]
    all_gather x5 -> x6, waiting for transfers between devices: 261 us -> 166 us  [the longest x1 50.9 us: on_device(): lax.all_gather(grad_down.astype(jnp.bfloat16), 'seq', axis=0, tiled=True)]
    concatenate x3 -> x4, other arithmetic: 74.6 us -> 2.25 us  [the longest x1 2.2 us: on_device(): jnp.concatenate([qkv_local, gain_rows], axis=0)]
    unnamed x2 -> x0, blocking collectives: 53 us -> none
    dot_general x7 -> x5, matrix products: 41.3 us -> 19.3 us  [contract_cols(): lax.dot_general(left_op, right_op, (((1,), (1,)), ((), ())), preferred_el...]
    all_gather x2 -> x0, blocking collectives: 21.7 us -> none  [the longest x1 11 us: on_device(): lax.all_gather(w_value, 'fsdp', axis=0, tiled=True)]
  transfers between devices with their start and end apart: 22 -> 20, of which waited for: 9 -> 12; matrix products, arithmetic and copies ran while one was open for 3% -> 24% of each run, Pallas kernels for 0% -> 0%
where the time goes in v1:
time: 619 us; the launch traced here: 613 us
  waiting for transfers between devices  382 us (62%)
  matrix products  83.9 us (14%)
  local copies, waits for them, and re-layouts  73.8 us (12%)
  other arithmetic  32 us (5%)
  starting transfers between devices  25.4 us (4%)
  between operations  15.3 us (2%)
    reduce_scatter x2, waiting for transfers between devices, row_sums(): lax.psum_scatter(partial.astype(jnp.bfloat16), 'seq', scatter_dimension=0...  79.5 us
    reduce_scatter x1, waiting for transfers between devices, on_device(): lax.psum_scatter(contract_rows(sum_left, sum_right).astype(jnp.bfloat16),...  54.6 us
    reduce_scatter x1, waiting for transfers between devices, on_device(): lax.psum_scatter(attn_sums, 'seq', scatter_dimension=0, tiled=True)  53.4 us
    all_gather x1, waiting for transfers between devices, on_device(): lax.all_gather(grad_down.astype(jnp.bfloat16), 'seq', axis=0, tiled=True)  50.9 us
    all_gather x1, waiting for transfers between devices, on_device(): lax.all_gather(ffn_scaled.astype(jnp.bfloat16), 'seq', axis=0, tiled=True)  49.9 us
    dot_general x8, matrix products, matmul(): return jnp.dot(left_op, right_op, preferred_element_type=jnp.float32)  32.2 us
    all_gather x1, waiting for transfers between devices, on_device(): gate_up = lax.all_gather(gate_up_local, 'fsdp', axis=0)  27.8 us
    dot_general x4, matrix products, contract_rows(): lax.dot_general(left_op, right_op, (((0,), (0,)), ((), ())), preferred_el...  27 us
  transfers between devices with their start and end apart: 20, of which 12 were waited for; matrix products, arithmetic and copies ran while one was open for 24% of the time, Pallas kernels for 0%

profile of v1, /device:TPU:0, one launch (start us, length us, event | category | flops | bytes accessed | tf_op | source)
XLA Modules:
  0.0 612.7 jit_solution(374237461409782764)
XLA Ops:
  7.2 4.2 concatenate.60
  20.8 27.0 %all-gather.17.cloned.1.call-done = bf16[1184,1536]{1,0:T(8,128)(2,1)} async-done(((bf16[296,1536]{1,0:T(8,128)(2,1)}), bf16[1184,1536]{1,0:T(8,128)(2,1)}) %all-gather.17.cloned.1.call-update) | async-done | bytes 3637264 | tf_op jit(solution)/shard_map/all_gather | solution.py:176
  58.4 4.3 collective-permute-start
  62.8 4.3 collective-permute-start.1
  82.0 27.8 %all-gather.19.cloned.1.call-done = bf16[8,288,864]{2,1,0:T(8,128)(2,1)} async-done(((bf16[2,288,864]{2,1,0:T(8,128)(2,1)}), bf16[8,288,864]{2,1,0:T(8,128)(2,1)}) %all-gather.19.cloned.1.call-update) | async-done | bytes 3981328 | tf_op jit(solution)/shard_map/all_gather | solution.py:201
  109.7 4.5 fusion.144
  114.3 49.9 %all-gather.11.cloned.1.call-done = bf16[1024,1152]{1,0:T(8,128)(2,1)} async-done(((bf16[128,1152]{1,0:T(8,128)(2,1)}), bf16[1024,1152]{1,0:T(8,128)(2,1)}) %all-gather.11.cloned.1.call-update) | async-done | bytes 2359312 | tf_op jit(solution)/shard_map/all_gather | solution.py:237
  164.2 5.0 fusion.152
  171.0 5.8 multiply_convert_fusion.1
  176.7 10.0 %all-gather.13.cloned.1.call-done = bf16[864,1152]{1,0:T(8,128)(2,1)} async-done(((bf16[216,1152]{1,0:T(8,128)(2,1)}), bf16[864,1152]{1,0:T(8,128)(2,1)}) %all-gather.13.cloned.1.call-update) | async-done | bytes 1990672 | tf_op jit(solution)/shard_map/all_gather | solution.py:204
  186.7 6.3 %convolution_convert_fusion.1 = bf16[1024,1152]{1,0:T(8,128)(2,1)} fusion(bf16[1024,864]{0,1:T(8,128)(2,1)} %get-tuple-element.22, bf16[864,1152]{1,0:T(8,128)(2,1)} %all-gather.13.cloned.1.call-done), kind=kOutput, calls=%fused_computation.14 | convolution fusion | flops 2039611392 | bytes 6119424 | tf_op jit(solution)/shard_map/dot_general | solution.py:116
  193.2 69.5 %reduce-scatter.6.cloned.1.call-done = bf16[128,1152]{1,0:T(8,128)(2,1)} async-done(((bf16[1024,1152]{1,0:T(8,128)(2,1)}), bf16[128,1152]{1,0:T(8,128)(2,1)}) %reduce-scatter.6.cloned.1.call-update) | async-done | bytes 294928 | tf_op jit(solution)/shard_map/reduce_scatter | solution.py:132
  267.5 50.9 %all-gather.15.cloned.1.call-done = bf16[1024,1152]{1,0:T(8,128)(2,1)} async-done(((bf16[128,1152]{1,0:T(8,128)(2,1)}), bf16[1024,1152]{1,0:T(8,128)(2,1)}) %all-gather.15.cloned.1.call-update) | async-done | bytes 2359312 | tf_op jit(solution)/shard_map/all_gather | solution.py:247
  318.4 9.1 %multiply_convert_fusion = (bf16[1024,864]{0,1:T(8,128)(2,1)S(1)}, bf16[1024,864]{0,1:T(8,128)(2,1)S(1)}) fusion(f32[1024,864]{0,1:T(8,128)} %copy-done.61, f32[1024,864]{0,1:T(8,128)} %get-tuple-element.93, bf16[1024,1152]{1,0:T(8,128)(2,1)} %all-gather.15.cloned.1.call-done, bf16[864,1152]{1,0:T(8,128)(2,1)} %all-gather.13.cloned.1.call-done), kind=kOutput, calls=%fused_computation.22 | convolution fusion | flops 2059665408 | bytes 14966784 | tf_op jit(solution)/shard_map/dot_general | solution.py:126
  330.5 4.3 add_convert_fusion
  335.3 6.8 %fusion.4 = bf16[1024,1280]{1,0:T(8,128)(2,1)} fusion(bf16[1024,1152]{1,0:T(8,128)(2,1)} %all-gather.11.cloned.1.call-done, s32[1280]{0:T(1024)S(1)} %fusion.124), kind=kOutput, calls=%fused_computation.12 | convolution fusion | flops 3022684160 | bytes 4985856 | tf_op jit(solution)/shard_map/dot_general | solution.py:116
  342.1 9.5 %convolution_convert_fusion.2 = bf16[1280,864]{0,1:T(8,128)(2,1)} fusion(bf16[1024,864]{0,1:T(8,128)(2,1)} %get-tuple-element.22, bf16[1024,1152]{1,0:T(8,128)(2,1)} %all-gather.15.cloned.1.call-done, s32[1280]{0:T(1024)S(1)} %fusion.124), kind=kOutput, calls=%fused_computation.24 | convolution fusion | flops 5288714240 | bytes 6345728 | tf_op jit(solution)/shard_map/dot_general | solution.py:120
  351.6 4.5 copy.180
  356.1 6.2 %convolution_convert_fusion.4 = bf16[1280,864]{0,1:T(8,128)(2,1)} fusion(bf16[1024,864]{0,1:T(8,128)(2,1)} %copy-done.62, bf16[1024,1280]{1,0:T(8,128)(2,1)} %fusion.4), kind=kOutput, calls=%fused_computation.26 | convolution fusion | flops 2266030080 | bytes 6602752 | tf_op jit(solution)/shard_map/dot_general | solution.py:120
  362.3 4.3 copy.178
  366.6 6.2 %convolution_convert_fusion.3 = bf16[1280,864]{0,1:T(8,128)(2,1)} fusion(bf16[1024,864]{0,1:T(8,128)(2,1)} %copy-done.64, bf16[1024,1280]{1,0:T(8,128)(2,1)} %fusion.4), kind=kOutput, calls=%fused_computation.25 | convolution fusion | flops 2266030080 | bytes 6602752 | tf_op jit(solution)/shard_map/dot_general | solution.py:120
  372.8 4.4 copy.179
  377.1 4.0 pad_maximum_fusion
  381.1 3.4 copy.181
  393.1 10.0 %reduce-scatter.8.cloned.1.call-done = bf16[128,1152]{1,0:T(8,128)(2,1)} async-done(((bf16[1024,1152]{1,0:T(8,128)(2,1)}), bf16[128,1152]{1,0:T(8,128)(2,1)}) %reduce-scatter.8.cloned.1.call-update) | async-done | bytes 294928 | tf_op jit(solution)/shard_map/reduce_scatter | solution.py:132
  430.2 4.8 collective-permute-done.4
  440.3 5.2 convolution_convert_fusion
  445.6 22.2 %reduce-scatter.14.cloned.1.call-done = bf16[960,864]{1,0:T(8,128)(2,1)} async-done(((bf16[3840,864]{1,0:T(8,128)(2,1)}), bf16[960,864]{1,0:T(8,128)(2,1)}) %reduce-scatter.14.cloned.1.call-update) | async-done | bytes 1658896 | tf_op jit(solution)/shard_map/reduce_scatter | solution.py:320
  470.6 5.7 all-to-all-start
  476.3 54.6 %reduce-scatter.10.cloned.1.call-done = bf16[320,2560]{1,0:T(8,128)(2,1)} async-done(((bf16[1280,2560]{1,0:T(8,128)(2,1)}), bf16[320,2560]{1,0:T(8,128)(2,1)}) %reduce-scatter.10.cloned.1.call-update) | async-done | bytes 1638416 | tf_op jit(solution)/shard_map/reduce_scatter | solution.py:357
  533.8 4.7 reshape.412
  546.8 53.4 %reduce-scatter.12.cloned.1.call-done = bf16[40,2560]{1,0:T(8,128)(2,1)} async-done(((bf16[320,2560]{1,0:T(8,128)(2,1)}), bf16[40,2560]{1,0:T(8,128)(2,1)}) %reduce-scatter.12.cloned.1.call-update) | async-done | bytes 204816 | tf_op jit(solution)/shard_map/reduce_scatter | solution.py:363
  (299 shorter events, 104.8 us)
Async XLA Ops:
  7.2 40.6 %all-gather.17.cloned.1.call-start = ((), (), s32[]{:S(2)}) async-start(), calls=%async_computation.15 | async-start | bytes 4546560 | tf_op jit(solution)/shard_map/all_gather | solution.py:176
  13.6 62.6 %all-gather.9.cloned.1.call-start = ((), (), s32[]{:S(2)}) async-start(), calls=%async_computation.6 | async-start | bytes 2949120 | tf_op jit(solution)/shard_map/all_gather | solution.py:186
  14.4 95.3 %all-gather.19.cloned.1.call-start = ((), (), s32[]{:S(2)}) async-start(), calls=%async_computation.16 | async-start | bytes 5160960 | tf_op jit(solution)/shard_map/all_gather | solution.py:201
  18.2 146.0 %all-gather.11.cloned.1.call-start = ((), (), s32[]{:S(2)}) async-start(), calls=%async_computation.7 | async-start | bytes 2654208 | tf_op jit(solution)/shard_map/all_gather | solution.py:237
  57.8 14.3 %copy-start.46 = (f32[4,64]{1,0:T(4,128)S(1)}, f32[4,64]{1,0:T(4,128)}, u32[]{:S(2)}) copy-start(f32[4,64]{1,0:T(4,128)} %get-tuple-element.80) | copy-start | bytes 3076
  57.9 14.2 %copy-start.47 = (f32[128]{0:T(128)}, f32[128]{0:T(128)S(1)}, u32[]{:S(2)}) copy-start(f32[128]{0:T(128)S(1)} %add_rsqrt_fusion.4) | copy-start | bytes 1540
  58.4 14.1 %copy-start.38 = (f32[4,288]{1,0:T(4,128)S(1)}, f32[4,288]{1,0:T(4,128)}, u32[]{:S(2)}) copy-start(f32[4,288]{1,0:T(4,128)} %get-tuple-element.78) | copy-start | bytes 13828
  58.4 14.1 %copy-start.37 = (f32[4,288]{1,0:T(4,128)S(1)}, f32[4,288]{1,0:T(4,128)}, u32[]{:S(2)}) copy-start(f32[4,288]{1,0:T(4,128)} %get-tuple-element.77) | copy-start | bytes 13828
  58.4 14.2 %collective-permute-start = (bf16[128,512]{1,0:T(8,128)(2,1)S(1)}, bf16[128,512]{1,0:T(8,128)(2,1)S(1)}, u32[]{:S(2)}, u32[]{:S(2)}) collective-permute-start(bf16[128,512]{1,0:T(8,128)(2,1)S(1)} %pad_maximum_fusion.7), channel_id=1, source_target_pairs={{0,16},{4,20},{8,24},{12,28},{1,17},{5,21},{9,25},{13,29},{2,18},{... | collective-permute-start | bytes 393224 | tf_op jit(solution)/shard_map/ppermute | solution.py:17
  62.8 9.9 %collective-permute-start.1 = (bf16[128,512]{1,0:T(8,128)(2,1)S(1)}, bf16[128,512]{1,0:T(8,128)(2,1)S(1)}, u32[]{:S(2)}, u32[]{:S(2)}) collective-permute-start(bf16[128,512]{1,0:T(8,128)(2,1)S(1)} %pad_maximum_fusion.7), channel_id=1, source_target_pairs={{0,12},{4,16},{8,20},{12,24},{16,28},{1,13},{5,17},{9,21},{13,25},... | collective-permute-start | bytes 393224 | tf_op jit(solution)/shard_map/ppermute | solution.py:17
  67.1 5.7 collective-permute-start.2
  68.4 5.7 collective-permute-start.3
  78.6 35.6 %copy-start.49 = (f32[128]{0:T(128)}, f32[128]{0:T(128)S(1)}, u32[]{:S(2)}) copy-start(f32[128]{0:T(128)S(1)} %add_rsqrt_fusion.3) | copy-start | bytes 1540
  78.9 35.3 %copy-start.51 = (f32[128]{0:T(128)}, f32[128]{0:T(128)S(1)}, u32[]{:S(2)}) copy-start(f32[128]{0:T(128)S(1)} %add_rsqrt_fusion.2) | copy-start | bytes 1540
  79.8 106.9 %all-gather.13.cloned.1.call-start = ((), (), s32[]{:S(2)}) async-start(), calls=%async_computation.8 | async-start | bytes 2488320 | tf_op jit(solution)/shard_map/all_gather | solution.py:204
  81.7 181.0 %reduce-scatter.6.cloned.1.call-start = ((), (), s32[]{:S(2)}) async-start(), calls=%async_computation.9 | async-start | bytes 2654208 | tf_op jit(solution)/shard_map/reduce_scatter | solution.py:132
  193.1 125.3 %all-gather.15.cloned.1.call-start = ((), (), s32[]{:S(2)}) async-start(), calls=%async_computation.10 | async-start | bytes 2654208 | tf_op jit(solution)/shard_map/all_gather | solution.py:247
  263.8 63.7 %copy-start.53 = (f32[128]{0:T(128)}, f32[128]{0:T(128)S(1)}, u32[]{:S(2)}) copy-start(f32[128]{0:T(128)S(1)} %add_rsqrt_fusion.1) | copy-start | bytes 1540
  267.2 135.9 %reduce-scatter.8.cloned.1.call-start = ((), (), s32[]{:S(2)}) async-start(), calls=%async_computation.11 | async-start | bytes 2654208 | tf_op jit(solution)/shard_map/reduce_scatter | solution.py:132
  334.8 132.9 %reduce-scatter.14.cloned.1.call-start = ((), (), s32[]{:S(2)}) async-start(), calls=%async_computation.14 | async-start | bytes 8601600 | tf_op jit(solution)/shard_map/reduce_scatter | solution.py:320
  384.6 146.2 %reduce-scatter.10.cloned.1.call-start = ((), (), s32[]{:S(2)}) async-start(), calls=%async_computation.12 | async-start | bytes 8192000 | tf_op jit(solution)/shard_map/reduce_scatter | solution.py:357
  387.3 15.8 %copy-start.52 = (f32[128]{0:T(128)S(1)}, f32[128]{0:T(128)}, u32[]{:S(2)}) copy-start(f32[128]{0:T(128)} %copy-done.51) | copy-start | bytes 1540
  388.3 16.1 %copy-start.50 = (f32[128]{0:T(128)S(1)}, f32[128]{0:T(128)}, u32[]{:S(2)}) copy-start(f32[128]{0:T(128)} %copy-done.49) | copy-start | bytes 1540
  388.3 16.1 %copy-start.54 = (f32[128]{0:T(128)S(1)}, f32[128]{0:T(128)}, u32[]{:S(2)}) copy-start(f32[128]{0:T(128)} %copy-done.53) | copy-start | bytes 1540
  421.3 13.7 %collective-permute-start.4 = (bf16[128,512]{1,0:T(8,128)(2,1)}, bf16[128,512]{1,0:T(8,128)(2,1)S(1)}, u32[]{:S(2)}, u32[]{:S(2)}) collective-permute-start(bf16[128,512]{1,0:T(8,128)(2,1)} %get-tuple-element.58), channel_id=1, source_target_pairs={{16,0},{20,4},{24,8},{28,12},{17,1},{21,5},{25,9},{29,13},{18,2},{... | collective-permute-start | bytes 393224 | tf_op jit(solution)/shard_map/ppermute | solution.py:17
  422.8 12.3 %collective-permute-start.5 = (bf16[128,512]{1,0:T(8,128)(2,1)}, bf16[128,512]{1,0:T(8,128)(2,1)}, u32[]{:S(2)}, u32[]{:S(2)}) collective-permute-start(bf16[128,512]{1,0:T(8,128)(2,1)} %get-tuple-element.61), channel_id=1, source_target_pairs={{12,0},{16,4},{20,8},{24,12},{28,16},{13,1},{17,5},{21,9},{25,13},... | collective-permute-start | bytes 393224 | tf_op jit(solution)/shard_map/ppermute | solution.py:17
  424.1 11.0 %collective-permute-start.6 = (bf16[128,512]{1,0:T(8,128)(2,1)}, bf16[128,512]{1,0:T(8,128)(2,1)}, u32[]{:S(2)}, u32[]{:S(2)}) collective-permute-start(bf16[128,512]{1,0:T(8,128)(2,1)} %get-tuple-element.60), channel_id=1, source_target_pairs={{8,0},{12,4},{16,8},{20,12},{24,16},{28,20},{9,1},{13,5},{17,9},{2... | collective-permute-start | bytes 393224 | tf_op jit(solution)/shard_map/ppermute | solution.py:17
  425.6 9.5 %collective-permute-start.7 = (bf16[128,512]{1,0:T(8,128)(2,1)}, bf16[128,512]{1,0:T(8,128)(2,1)}, u32[]{:S(2)}, u32[]{:S(2)}) collective-permute-start(bf16[128,512]{1,0:T(8,128)(2,1)} %get-tuple-element.59), channel_id=1, source_target_pairs={{4,0},{8,4},{12,8},{16,12},{20,16},{24,20},{28,24},{5,1},{9,5},{13... | collective-permute-start | bytes 393224 | tf_op jit(solution)/shard_map/ppermute | solution.py:17
  470.5 60.3 %copy-start.6 = (f32[128,1152]{1,0:T(8,128)S(1)}, f32[128,1152]{1,0:T(8,128)}, u32[]{:S(2)}) copy-start(f32[128,1152]{1,0:T(8,128)} %copy-done.5) | copy-start | bytes 1769476
  470.6 60.3 %copy-start.27 = (f32[128,1152]{1,0:T(8,128)S(1)}, f32[128,1152]{1,0:T(8,128)}, u32[]{:S(2)}) copy-start(f32[128,1152]{1,0:T(8,128)} %get-tuple-element.94) | copy-start | bytes 1769476
  470.6 61.4 %all-to-all-start = ((bf16[3,8,40,864]{3,2,0,1:T(8,128)(2,1)}), bf16[3,8,40,864]{3,2,0,1:T(8,128)(2,1)S(1)}, u32[]{:S(2)}, u32[]{:S(2)}) async-start(bf16[3,8,40,864]{3,2,0,1:T(8,128)(2,1)} %copy.182), calls=%async_computation.5 | async-start | bytes 3440640 | tf_op jit(solution)/shard_map/all_to_all | solution.py:321
  476.2 124.0 %reduce-scatter.12.cloned.1.call-start = ((), (), s32[]{:S(2)}) async-start(), calls=%async_computation.13 | async-start | bytes 1843200 | tf_op jit(solution)/shard_map/reduce_scatter | solution.py:363
  (53 other events, 248.0 us)
Sparse Core Ops, SparseCore 0:
  13.8 34.0 all-gather.16
  49.4 24.0 all-gather.8
  75.6 34.0 all-gather.18
  112.3 51.7 all-gather.10
  166.2 20.4 all-gather.12
  193.2 69.4 reduce-scatter.5
  267.4 50.9 all-gather.14
  335.0 68.0 reduce-scatter.7
  405.6 62.0 reduce-scatter.13
  470.1 60.6 reduce-scatter.9
  534.3 65.8 reduce-scatter.11
